TPU v7x, 32 devices: a whole 2x2x4 slice. The times are simulated.
32 devices in a mesh: grp: 2 (over y), seq: 4 (over z), head: 2 (over x), clip: 2 (over core).
Axes of the slice: x: 2, y: 2, z: 4, core: 2. Of those that a mesh axis runs over, the one named last changes fastest.
Arguments:
- query_states: bfloat16 [4, 2048, 1536], P(('grp', 'clip'), 'seq', 'head'), parts along dimension 0, may hold values from -64 to 64
- key_states: bfloat16 [4, 2048, 1536], P(('grp', 'clip'), 'seq', 'head'), parts along dimension 0, may hold values from -4 to 4
- value_states: bfloat16 [4, 2048, 1536], P(('grp', 'clip'), 'seq', 'head'), parts along dimension 0, may hold values from -5 to 5
- output_grad: bfloat16 [4, 2048, 3072], P(('grp', 'clip'), 'seq', 'head'), parts along dimension 0, may hold values from -48 to 48
- w_out: bfloat16 [1536, 3072], P('head'), may hold values from -0.15625 to 0.15625
- key_list: int32 [4, 8, 8], P(('grp', 'clip')), parts along dimension 0, may hold values from 0 to 7, as said below
- key_count: int32 [4, 8], P(('grp', 'clip')), parts along dimension 0, may hold values from 1 to 8, as said below
Outputs:
- query_grad: bfloat16 [4, 2048, 1536], P(('grp', 'clip'), 'seq', 'head'), parts along dimension 0
- key_grad: bfloat16 [4, 2048, 1536], P(('grp', 'clip'), 'seq', 'head'), parts along dimension 0
- value_grad: bfloat16 [4, 2048, 1536], P(('grp', 'clip'), 'seq', 'head'), parts along dimension 0
- grad_features: float32 [4, 12, 3], P(('grp', 'clip'), 'head'), parts along dimension 0
There are 2 independent parts, one for each index of `grp`. A program takes and returns all parts, laid end to end along the dimension named above; an argument that names none is the same for every part. Nothing has to cross between parts.
Inputs may be any that keep to these rules, and one draw needn't show every extreme that they name: Tile i lies in frame block i // 4 at place i % 4. For each clip and query tile i the first key_count entries of key_list are distinct key tiles in ascending order, among them i itself, each at a place within 2 of i's place, in i's frame block or in the other one; the remaining entries equal i. `key_count`: in every draw some query tile lists 8 key tiles.
All inputs are finite; a program needn't handle non-finite values.
Results may differ from a plain program's by a relative error of at most 0.035.
Values may be sent and summed in bfloat16 or wider, within the bound.
No kernel may reach another device: no remote copies, remote signals or barrier semaphores. Data moves between devices by JAX's collectives and lax.ppermute only.
A program may use at most 128 MiB of HBM per device.

v0:
```python
import jax
import jax.numpy as jnp
from jax import lax
from jax.sharding import PartitionSpec as P

HD = 128
TILE = 256


def attend(query_tiles, key_buf, value_buf, grad_tiles, buf_slots, counts):
    score_scale = HD ** (-0.5)
    tile_count, tile_rows, feat_width = query_tiles.shape
    slot_count = buf_slots.shape[1]
    key_span = slot_count * tile_rows
    buf_tiles = key_buf.shape[0]
    key_sel = key_buf[buf_slots].reshape(tile_count, key_span, feat_width)
    value_sel = value_buf[buf_slots].reshape(tile_count, key_span, feat_width)
    allowed = jnp.arange(key_span)[None, :] // tile_rows < counts[:, None]

    def head_step(head_idx, carried):
        query_acc, key_acc, value_acc = carried
        col_start = head_idx * HD
        query_head = lax.dynamic_slice_in_dim(query_tiles, col_start, HD, 2)
        key_head = lax.dynamic_slice_in_dim(key_sel, col_start, HD, 2)
        value_head = lax.dynamic_slice_in_dim(value_sel, col_start, HD, 2)
        grad_head = lax.dynamic_slice_in_dim(grad_tiles, col_start, HD, 2)
        scores = (
            jnp.einsum("iqe,ike->iqk", query_head, key_head, preferred_element_type=jnp.float32)
            * score_scale
        )
        scores = jnp.where(allowed[:, None, :], scores, -jnp.inf)
        row_max = jnp.max(scores, axis=-1, keepdims=True)
        log_norm = row_max + jnp.log(jnp.sum(jnp.exp(scores - row_max), axis=-1, keepdims=True))
        weights = jnp.exp(scores - log_norm)
        weights_b = weights.astype(jnp.bfloat16)
        attn_out = jnp.einsum(
            "iqk,ike->iqe", weights_b, value_head, preferred_element_type=jnp.float32
        ).astype(jnp.bfloat16)
        row_delta = jnp.sum(
            grad_head.astype(jnp.float32) * attn_out.astype(jnp.float32), axis=-1, keepdims=True
        )
        dprob = jnp.einsum(
            "iqe,ike->iqk", grad_head, value_head, preferred_element_type=jnp.float32
        )
        dscore = (weights * (dprob - row_delta)).astype(jnp.bfloat16)
        query_head_grad = score_scale * jnp.einsum(
            "iqk,ike->iqe", dscore, key_head, preferred_element_type=jnp.float32
        )
        key_head_grad = score_scale * jnp.einsum(
            "iqk,iqe->ike", dscore, query_head, preferred_element_type=jnp.float32
        )
        value_head_grad = jnp.einsum(
            "iqk,iqe->ike", weights_b, grad_head, preferred_element_type=jnp.float32
        )
        query_acc = lax.dynamic_update_slice_in_dim(query_acc, query_head_grad, col_start, 2)
        key_acc = lax.dynamic_update_slice_in_dim(key_acc, key_head_grad, col_start, 2)
        value_acc = lax.dynamic_update_slice_in_dim(value_acc, value_head_grad, col_start, 2)
        return (query_acc, key_acc, value_acc)

    start_state = (
        jnp.zeros((tile_count, tile_rows, feat_width), jnp.float32),
        jnp.zeros((tile_count, key_span, feat_width), jnp.float32),
        jnp.zeros((tile_count, key_span, feat_width), jnp.float32),
    )
    query_full, key_sel_grad, value_sel_grad = lax.fori_loop(
        0, feat_width // HD, head_step, start_state
    )
    live_slot = jnp.arange(slot_count)[None, :] < counts[:, None]
    routing = (
        (buf_slots[:, :, None] == jnp.arange(buf_tiles)[None, None, :]) & live_slot[:, :, None]
    ).astype(jnp.float32)
    key_grad_buf = jnp.einsum(
        "imb,imr->br",
        routing,
        key_sel_grad.reshape(tile_count, slot_count, tile_rows * feat_width),
        precision=lax.Precision.HIGHEST,
    )
    value_grad_buf = jnp.einsum(
        "imb,imr->br",
        routing,
        value_sel_grad.reshape(tile_count, slot_count, tile_rows * feat_width),
        precision=lax.Precision.HIGHEST,
    )
    return (
        query_full,
        key_grad_buf.reshape(buf_tiles, tile_rows, feat_width),
        value_grad_buf.reshape(buf_tiles, tile_rows, feat_width),
    )


def head_squares(grads_full, head_count):
    rows = grads_full.reshape(-1, head_count, HD)
    return jnp.sum(rows * rows, axis=(0, 2))


def per_device(query_states, key_states, value_states, output_grad, w_out, key_list, key_count):
    seq_count = lax.axis_size("seq")
    seq_index = lax.axis_index("seq")
    tok_rows = query_states.shape[1]
    feat_width = query_states.shape[2]
    head_count = feat_width // HD
    tile_count = tok_rows // TILE
    first_tile = seq_index * tile_count
    own_lists = lax.dynamic_slice_in_dim(key_list[0], first_tile, tile_count, 0)
    own_counts = lax.dynamic_slice_in_dim(key_count[0], first_tile, tile_count, 0)
    grad_out = lax.dot_general(
        lax.all_gather(output_grad, "head", axis=2, tiled=True)[0],
        w_out,
        (((1,), (1,)), ((), ())),
        preferred_element_type=jnp.float32,
    ).astype(jnp.bfloat16)
    query_tiles = query_states[0].reshape(tile_count, TILE, feat_width)
    grad_tiles = grad_out.reshape(tile_count, TILE, feat_width)
    key_whole, value_whole = (
        lax.all_gather(key_states, "seq", axis=1, tiled=True),
        lax.all_gather(value_states, "seq", axis=1, tiled=True),
    )
    key_buf = key_whole[0].reshape(-1, TILE, feat_width)
    value_buf = value_whole[0].reshape(-1, TILE, feat_width)
    query_full, key_grad_buf, value_grad_buf = attend(
        query_tiles, key_buf, value_buf, grad_tiles, own_lists, own_counts
    )
    buf_rows = key_grad_buf.shape[0] * TILE
    key_sum, value_sum = (
        lax.psum_scatter(
            key_grad_buf.reshape(1, buf_rows, feat_width).astype(jnp.bfloat16),
            "seq",
            scatter_dimension=1,
            tiled=True,
        ).astype(jnp.float32),
        lax.psum_scatter(
            value_grad_buf.reshape(1, buf_rows, feat_width).astype(jnp.bfloat16),
            "seq",
            scatter_dimension=1,
            tiled=True,
        ).astype(jnp.float32),
    )
    key_full = key_sum[0]
    value_full = value_sum[0]
    query_rows = query_full.reshape(tok_rows, feat_width)
    local_sums = jnp.stack(
        [
            head_squares(query_rows, head_count),
            head_squares(key_full, head_count),
            head_squares(value_full, head_count),
        ],
        axis=-1,
    )
    total_sums = lax.psum(local_sums, "seq")
    grad_features = jnp.log(total_sums / (seq_count * tok_rows * HD) + 1e-06)
    return (
        query_rows.astype(jnp.bfloat16)[None],
        key_full.astype(jnp.bfloat16)[None],
        value_full.astype(jnp.bfloat16)[None],
        grad_features[None],
    )


def solution(mesh):
    in_specs = (
        P(("grp", "clip"), "seq", "head"),
        P(("grp", "clip"), "seq", "head"),
        P(("grp", "clip"), "seq", "head"),
        P(("grp", "clip"), "seq", "head"),
        P("head", None),
        P(("grp", "clip"), None, None),
        P(("grp", "clip"), None),
    )
    out_specs = (
        P(("grp", "clip"), "seq", "head"),
        P(("grp", "clip"), "seq", "head"),
        P(("grp", "clip"), "seq", "head"),
        P(("grp", "clip"), "head", None),
    )
    return jax.shard_map(
        per_device, mesh=mesh, in_specs=in_specs, out_specs=out_specs, check_vma=False
    )
```

profile of v0, /device:TPU:0, one launch (start us, length us, event | category | flops | bytes accessed | tf_op | source)
XLA Modules:
  0.0 461.2 jit_solution(8411246772068753391)
XLA Ops:
  11.1 46.2 %all-gather.6.cloned.1.call-done = bf16[1,512,3072]{2,1,0:T(8,128)(2,1)} async-done(((bf16[1,512,1536]{2,1,0:T(8,128)(2,1)}), bf16[1,512,3072]{2,1,0:T(8,128)(2,1)}) %all-gather.6.cloned.1.call-update) | async-done | bytes 3145744 | tf_op jit(solution)/shard_map/all_gather | solution.py:107
  57.3 5.9 %fusion.28 = bf16[512,768]{1,0:T(8,128)(2,1)S(1)} fusion(bf16[768,3072]{1,0:T(8,128)(2,1)} %param.13, bf16[1,512,3072]{2,1,0:T(8,128)(2,1)} %all-gather.6.cloned.1.call-done), kind=kOutput, calls=%fused_computation.42 | convolution fusion | flops 2416312320 | bytes 8650752 | tf_op jit(solution)/shard_map/dot_general | solution.py:106
  63.2 59.1 %all-gather.4.cloned.1.call-done = bf16[1,2048,768]{2,1,0:T(8,128)(2,1)} async-done(((bf16[1,512,768]{2,1,0:T(8,128)(2,1)}), bf16[1,2048,768]{2,1,0:T(8,128)(2,1)}) %all-gather.4.cloned.1.call-update) | async-done | bytes 3145744 | tf_op jit(solution)/shard_map/all_gather | solution.py:115
  122.3 5.6 %gather_fusion = bf16[16,256,768]{2,1,0:T(8,128)(2,1)} fusion(bf16[8,256,768]{2,1,0:T(8,128)(2,1)} %bitcast.50, s32[1024]{0:T(1024)S(1)} %pad_clamp_fusion), kind=kCustom, calls=%fused_computation | custom fusion | bytes 12582976 | tf_op jit(solution)/shard_map/gather | solution.py:16
  127.9 58.1 %all-gather.8.cloned.1.call-done = bf16[1,2048,768]{2,1,0:T(8,128)(2,1)} async-done(((bf16[1,512,768]{2,1,0:T(8,128)(2,1)}), bf16[1,2048,768]{2,1,0:T(8,128)(2,1)}) %all-gather.8.cloned.1.call-update) | async-done | bytes 3145744 | tf_op jit(solution)/shard_map/all_gather | solution.py:116
  186.0 5.5 %gather_fusion.1 = bf16[16,256,768]{2,1,0:T(8,128)(2,1)} fusion(bf16[8,256,768]{2,1,0:T(8,128)(2,1)} %bitcast.51, s32[1024]{0:T(1024)S(1)} %pad_clamp_fusion), kind=kCustom, calls=%fused_computation.1 | custom fusion | bytes 12582976 | tf_op jit(solution)/shard_map/gather | solution.py:17
  191.5 5.4 %broadcast.103 = f32[2,2048,768]{2,1,0:T(8,128)} broadcast(f32[]{:T(128)} %constant.78.clone.1), dimensions={} | broadcast | bytes 12582916 | tf_op jit(solution)/shard_map/broadcast.13
  196.9 5.3 %broadcast.103.clone = f32[2,2048,768]{2,1,0:T(8,128)} broadcast(f32[]{:T(128)} %constant.78.clone.1), dimensions={} | broadcast | bytes 12582916 | tf_op jit(solution)/shard_map/broadcast.13
  202.3 92.5 %while.18 = (s32[]{:T(128)}, f32[2,256,768]{2,1,0:T(8,128)S(1)}, f32[2,2048,768]{2,1,0:T(8,128)}, f32[2,2048,768]{2,1,0:T(8,128)}, bf16[2,256,768]{2,1,0:T(8,128...) while((s32[]{:T(128)}, f32[2,256,768]{2,1,0:T(8,128)S(1)}, ...), condition=%wide.region_4.5_spmd.clone, body=%wide.region_0.4_spmd.clone.sunk | while | flops 1625164800 | bytes 36614328 | solution.py:65
  202.6 2.1 fusion.71
  204.7 0.7 exponential_reduce_fusion.2
  205.4 2.6 convolution_dynamic-update-slice_fusion.2
  208.0 2.2 fusion.72
  210.2 2.3 multiply_convert_fusion.2
  212.5 3.4 fusion.74
  215.9 1.9 fusion.73
  217.9 2.1 fusion.71
  220.0 0.7 exponential_reduce_fusion.2
  220.8 2.6 convolution_dynamic-update-slice_fusion.2
  223.4 2.2 fusion.72
  225.6 2.3 multiply_convert_fusion.2
  227.9 3.3 fusion.74
  231.2 1.9 fusion.73
  233.3 2.1 fusion.71
  235.4 0.7 exponential_reduce_fusion.2
  236.1 2.7 convolution_dynamic-update-slice_fusion.2
  238.8 2.2 fusion.72
  240.9 2.3 multiply_convert_fusion.2
  243.2 3.3 fusion.74
  246.6 1.9 fusion.73
  248.6 2.1 fusion.71
  250.7 0.7 exponential_reduce_fusion.2
  251.5 2.8 convolution_dynamic-update-slice_fusion.2
  254.2 2.2 fusion.72
  256.4 2.3 multiply_convert_fusion.2
  258.7 3.4 fusion.74
  262.1 1.9 fusion.73
  264.1 2.1 fusion.71
  267.0 2.7 convolution_dynamic-update-slice_fusion.2
  269.7 2.2 fusion.72
  271.8 2.3 multiply_convert_fusion.2
  274.1 3.4 fusion.74
  277.5 1.9 fusion.73
  279.6 2.1 fusion.71
  281.7 0.7 exponential_reduce_fusion.2
  282.4 2.6 convolution_dynamic-update-slice_fusion.2
  285.0 2.2 fusion.72
  287.2 2.3 multiply_convert_fusion.2
  289.5 3.4 fusion.74
  292.8 1.9 fusion.73
  294.8 1.1 copy-done.2
  295.9 13.2 %reshape.176 = f32[2,8,196608]{2,1,0:T(8,128)} reshape(f32[2,2048,768]{2,1,0:T(8,128)} %get-tuple-element.161) | data formatting | bytes 25165824 | tf_op jit(solution)/shard_map/reshape | solution.py:75
  309.2 7.6 %fusion.24 = bf16[8,196608]{1,0:T(8,128)(2,1)S(1)} fusion(f32[2,8,196608]{2,1,0:T(8,128)} %reshape.176, s32[2,8]{1,0:T(2,128)S(1)} %dynamic-slice_bitcast_fusion, pred[2,8]{1,0:T(4,128)(4,1)S(1)} %iota_compare_fusion.1), kind=kOutput, calls=%fused_computation.35 | convolution fusion | flops 303563008 | bytes 15728720 | tf_op jit(solution)/shard_map/imb,imr->br/dot_general | solution.py:72
  316.8 3.2 convert_element_type.94
  320.0 13.3 %reshape.177 = f32[2,8,196608]{2,1,0:T(8,128)} reshape(f32[2,2048,768]{2,1,0:T(8,128)} %get-tuple-element.162) | data formatting | bytes 25165824 | tf_op jit(solution)/shard_map/reshape | solution.py:81
  333.3 7.6 %fusion.25 = bf16[8,196608]{1,0:T(8,128)(2,1)S(1)} fusion(f32[2,8,196608]{2,1,0:T(8,128)} %reshape.177, s32[2,8]{1,0:T(2,128)S(1)} %dynamic-slice_bitcast_fusion, pred[2,8]{1,0:T(4,128)(4,1)S(1)} %iota_compare_fusion.1), kind=kOutput, calls=%fused_computation.36 | convolution fusion | flops 303563008 | bytes 15728720 | tf_op jit(solution)/shard_map/imb,imr->br/dot_general | solution.py:78
  341.0 3.1 convert_element_type.96
  344.1 1.4 copy-done.3
  345.5 1.0 multiply_reduce_fusion.2
  346.6 32.6 %reduce-scatter.3.cloned.1.call-done = bf16[1,512,768]{2,1,0:T(8,128)(2,1)} async-done(((bf16[1,2048,768]{2,1,0:T(8,128)(2,1)}), bf16[1,512,768]{2,1,0:T(8,128)(2,1)}) %reduce-scatter.3.cloned.1.call-update) | async-done | bytes 786448 | tf_op jit(solution)/shard_map/reduce_scatter | solution.py:125
  379.2 1.3 multiply_reduce_fusion.1
  380.6 61.6 %reduce-scatter.5.cloned.1.call-done = bf16[1,512,768]{2,1,0:T(8,128)(2,1)} async-done(((bf16[1,2048,768]{2,1,0:T(8,128)(2,1)}), bf16[1,512,768]{2,1,0:T(8,128)(2,1)}) %reduce-scatter.5.cloned.1.call-update) | async-done | bytes 786448 | tf_op jit(solution)/shard_map/reduce_scatter | solution.py:131
  442.2 1.3 multiply_reduce_fusion
  443.7 10.4 %psum.7 = f32[6,3]{0,1:T(4,128)S(1)} all-reduce(f32[6,3]{0,1:T(4,128)S(1)} %pad_maximum_fusion), channel_id=1, replica_groups=mesh['grp'=2,'seq'=4,'head'=2,'clip'=2] {'seq'}, use_global_device_ids=true, to_apply=%region_13.14 | all-reduce | flops 18 | bytes 144 | tf_op jit(solution)/shard_map/psum | solution.py:149
  (43 shorter events, 6.2 us)
Async XLA Ops:
  7.2 3.1 copy-start
  7.2 50.1 %all-gather.6.cloned.1.call-start = ((), (), s32[]{:S(2)}) async-start(), calls=%async_computation.3 | async-start | bytes 4718592 | tf_op jit(solution)/shard_map/all_gather | solution.py:107
  7.9 114.4 %all-gather.4.cloned.1.call-start = ((), (), s32[]{:S(2)}) async-start(), calls=%async_computation.2 | async-start | bytes 3932160 | tf_op jit(solution)/shard_map/all_gather | solution.py:115
  8.7 177.3 %all-gather.8.cloned.1.call-start = ((), (), s32[]{:S(2)}) async-start(), calls=%async_computation.4 | async-start | bytes 3932160 | tf_op jit(solution)/shard_map/all_gather | solution.py:116
  9.4 369.8 %reduce-scatter.3.cloned.1.call-start = ((), (), s32[]{:S(2)}) async-start(), calls=%async_computation.5 | async-start | bytes 3932160 | tf_op jit(solution)/shard_map/reduce_scatter | solution.py:125
  294.8 1.1 copy-start.2
  320.0 122.3 %reduce-scatter.5.cloned.1.call-start = ((), (), s32[]{:S(2)}) async-start(), calls=%async_computation.6 | async-start | bytes 3932160 | tf_op jit(solution)/shard_map/reduce_scatter | solution.py:131
  340.9 113.7 %copy-start.1 = (s32[1,8]{1,0:T(1,128)S(1)}, s32[1,8]{1,0:T(1,128)}, u32[]{:S(2)}) copy-start(s32[1,8]{1,0:T(1,128)} %param.15) | copy-start | bytes 100
  344.0 1.4 copy-start.3
Sparse Core Ops, SparseCore 0:
  9.5 47.6 all-gather.5
  58.8 63.4 all-gather.3
  123.9 62.0 all-gather.7
  320.1 59.0 reduce-scatter.2
  381.9 60.3 reduce-scatter.4
where the time goes:
time: 463 us; the launch traced here: 461 us
  waiting for transfers between devices  260 us (56%)
  matrix products  108 us (23%)
  local copies, waits for them, and re-layouts  58.6 us (13%)
  between operations  13.9 us (3%)
  blocking collectives  10.4 us (2%)
  other arithmetic  9.63 us (2%)
    reduce_scatter x1, waiting for transfers between devices, per_device(): lax.psum_scatter(value_grad_buf.reshape(1, buf_rows, feat_width).astype(j...  61.6 us
    all_gather x1, waiting for transfers between devices, per_device(): lax.all_gather(key_states, 'seq', axis=1, tiled=True)  59.1 us
    all_gather x1, waiting for transfers between devices, per_device(): lax.all_gather(value_states, 'seq', axis=1, tiled=True)  58.1 us
    all_gather x1, waiting for transfers between devices, per_device(): lax.all_gather(output_grad, 'head', axis=2, tiled=True)[0]  46.2 us
    reduce_scatter x1, waiting for transfers between devices, per_device(): lax.psum_scatter(key_grad_buf.reshape(1, buf_rows, feat_width).astype(jnp...  32.6 us
    dot_general x6, matrix products, head_step(): jnp.einsum('iqk,iqe->ike', dscore, query_head, preferred_element_type=jnp...  20.2 us
    dot_general x6, matrix products, head_step(): jnp.einsum('iqk,iqe->ike', weights_b, grad_head, preferred_element_type=j...  16 us
    dot_general x6, matrix products, head_step(): jnp.einsum('iqe,ike->iqk', grad_head, value_head, preferred_element_type=...  13.7 us
  transfers between devices with their start and end apart: 5, of which 5 were waited for; matrix products, arithmetic and copies ran while one was open for 9% of the time, Pallas kernels for 0%

commit v1 on v0

--- a/solution.py
+++ b/solution.py
@@ -1,3 +1,4 @@
+import functools
 import jax
 import jax.numpy as jnp
 from jax import lax
@@ -5,6 +6,34 @@
 
 HD = 128
 TILE = 256
+
+
+def put_units(w_in, peer_axis):
+    z1 = jax.lax.axis_size(peer_axis)
+    response = jax.lax.axis_index(peer_axis)
+    part_now, high, f_next = (z1, response, w_in.shape[1])
+    found = [(src_i, (src_i + 1) % part_now) for src_i in range(part_now)]
+    buffer = [(src_i, (src_i - 1) % part_now) for src_i in range(part_now)]
+    after = jnp.zeros((*w_in.shape[:1], part_now * f_next, *w_in.shape[2:]), w_in.dtype)
+    after = lax.dynamic_update_slice_in_dim(after, w_in, high * f_next, axis=1)
+    state_now = f_now = w_in
+    s_next = part_now // 2
+    t = 1
+    while t < s_next + 1:
+        state_now = jax.lax.ppermute(state_now, peer_axis, perm=found)
+        after = lax.dynamic_update_slice_in_dim(
+            after, state_now, (high - t) % part_now * f_next, axis=1
+        )
+        if t < part_now - s_next:
+            f_now = jax.lax.ppermute(f_now, peer_axis, perm=buffer)
+            after = lax.dynamic_update_slice_in_dim(
+                after, f_now, (high + t) % part_now * f_next, axis=1
+            )
+        t += 1
+    return after
+
+
+see_matrix = functools.partial(put_units, peer_axis="seq")
 
 
 def attend(query_tiles, key_buf, value_buf, grad_tiles, buf_slots, counts):
@@ -113,7 +142,7 @@
     grad_tiles = grad_out.reshape(tile_count, TILE, feat_width)
     key_whole, value_whole = (
         lax.all_gather(key_states, "seq", axis=1, tiled=True),
-        lax.all_gather(value_states, "seq", axis=1, tiled=True),
+        see_matrix(value_states),
     )
     key_buf = key_whole[0].reshape(-1, TILE, feat_width)
     value_buf = value_whole[0].reshape(-1, TILE, feat_width)

time: 463 us -> 399 us (0.86)
  waiting for transfers between devices: 260 us -> 188 us
  starting transfers between devices: 0.19 us -> 5.36 us
    all_gather x1 -> x0, waiting for transfers between devices: 58.1 us -> none  [per_device(): lax.all_gather(value_states, 'seq', axis=1, tiled=True)]
    all_gather x1, waiting for transfers between devices: 46.2 us -> 0.01 us  [per_device(): lax.all_gather(output_grad, 'head', axis=2, tiled=True)[0]]
    ppermute x0 -> x3, waiting for transfers between devices: none -> 46.1 us  [the longest x2 33.2 us: put_units(): state_now = jax.lax.ppermute(state_now, peer_axis, perm=found)]
    all_gather x1, waiting for transfers between devices: 59.1 us -> 45.9 us  [per_device(): lax.all_gather(key_states, 'seq', axis=1, tiled=True)]
    ppermute x0 -> x3, starting transfers between devices: none -> 5.2 us  [the longest x2 3.11 us: put_units(): state_now = jax.lax.ppermute(state_now, peer_axis, perm=found)]
    dynamic_update_slice x0 -> x4, local copies, waits for them, and re-layouts: none -> 4.83 us  [the longest x2 2.45 us: put_units(): lax.dynamic_update_slice_in_dim(after, state_now, (high - t) % part_now *...]
  transfers between devices with their start and end apart: 5 -> 7, of which waited for: 5 -> 6; matrix products, arithmetic and copies ran while one was open for 9% -> 11% of each run, Pallas kernels for 0% -> 0%
where the time goes in v1:
time: 399 us; the launch traced here: 397 us
  waiting for transfers between devices  188 us (47%)
  matrix products  108 us (27%)
  local copies, waits for them, and re-layouts  61.8 us (15%)
  between operations  13.9 us (3%)
  blocking collectives  10.4 us (3%)
  other arithmetic  9.63 us (2%)
  starting transfers between devices  5.36 us (1%)
    reduce_scatter x1, waiting for transfers between devices, per_device(): lax.psum_scatter(value_grad_buf.reshape(1, buf_rows, feat_width).astype(j...  61.6 us
    all_gather x1, waiting for transfers between devices, per_device(): lax.all_gather(key_states, 'seq', axis=1, tiled=True)  45.9 us
    ppermute x2, waiting for transfers between devices, put_units(): state_now = jax.lax.ppermute(state_now, peer_axis, perm=found)  33.2 us
    reduce_scatter x1, waiting for transfers between devices, per_device(): lax.psum_scatter(key_grad_buf.reshape(1, buf_rows, feat_width).astype(jnp...  32.6 us
    dot_general x6, matrix products, head_step(): jnp.einsum('iqk,iqe->ike', dscore, query_head, preferred_element_type=jnp...  20.2 us
    dot_general x6, matrix products, head_step(): jnp.einsum('iqk,iqe->ike', weights_b, grad_head, preferred_element_type=j...  16 us
    dot_general x6, matrix products, head_step(): jnp.einsum('iqe,ike->iqk', grad_head, value_head, preferred_element_type=...  13.7 us
    reshape x1, local copies, waits for them, and re-layouts, attend(): value_sel_grad.reshape(tile_count, slot_count, tile_rows * feat_width)  13.3 us
  transfers between devices with their start and end apart: 7, of which 6 were waited for; matrix products, arithmetic and copies ran while one was open for 11% of the time, Pallas kernels for 0%

profile of v1, /device:TPU:0, one launch (start us, length us, event | category | flops | bytes accessed | tf_op | source)
XLA Modules:
  0.0 397.4 jit_solution(441169688991225653)
XLA Ops:
  8.7 3.1 collective-permute-start
  11.8 2.1 collective-permute-start.1
  15.4 17.2 %collective-permute-done = bf16[1,512,768]{2,1,0:T(8,128)(2,1)} collective-permute-done((bf16[1,512,768]{2,1,0:T(8,128)(2,1)}, bf16[1,512,768]{2,1,0:T(8,128)(2,1)}, u32[]{:S(2)}, u32[]{:S(2)}) %collective-permute-start) | collective-permute-done | bytes 786464 | tf_op jit(solution)/shard_map/ppermute | solution.py:23
  32.9 1.2 constant_dynamic-update-slice_fusion.3
  34.2 1.2 constant_dynamic-update-slice_fusion.2
  35.4 12.9 %collective-permute-done.1 = bf16[1,512,768]{2,1,0:T(8,128)(2,1)} collective-permute-done((bf16[1,512,768]{2,1,0:T(8,128)(2,1)}, bf16[1,512,768]{2,1,0:T(8,128)(2,1)}, u32[]{:S(2)}, u32[]{:S(2)}) %collective-permute-start.1) | collective-permute-done | bytes 786464 | tf_op jit(solution)/shard_map/ppermute | solution.py:28
  48.2 1.2 constant_dynamic-update-slice_fusion.1
  49.4 16.0 %collective-permute-done.2 = bf16[1,512,768]{2,1,0:T(8,128)(2,1)} collective-permute-done((bf16[1,512,768]{2,1,0:T(8,128)(2,1)}, bf16[1,512,768]{2,1,0:T(8,128)(2,1)}, u32[]{:S(2)}, u32[]{:S(2)}) %collective-permute-start.2) | collective-permute-done | bytes 786464 | tf_op jit(solution)/shard_map/ppermute | solution.py:23
  65.5 1.3 constant_dynamic-update-slice_fusion
  66.7 3.7 gather_fusion.1
  70.4 5.9 %fusion.28 = bf16[512,768]{1,0:T(8,128)(2,1)S(1)} fusion(bf16[768,3072]{1,0:T(8,128)(2,1)} %param.13, bf16[1,512,3072]{2,1,0:T(8,128)(2,1)} %all-gather.5.cloned.1.call-done), kind=kOutput, calls=%fused_computation.42 | convolution fusion | flops 2416312320 | bytes 8650752 | tf_op jit(solution)/shard_map/dot_general | solution.py:135
  76.3 45.9 %all-gather.3.cloned.1.call-done = bf16[1,2048,768]{2,1,0:T(8,128)(2,1)} async-done(((bf16[1,512,768]{2,1,0:T(8,128)(2,1)}), bf16[1,2048,768]{2,1,0:T(8,128)(2,1)}) %all-gather.3.cloned.1.call-update) | async-done | bytes 3145744 | tf_op jit(solution)/shard_map/all_gather | solution.py:144
  122.2 5.5 %gather_fusion = bf16[16,256,768]{2,1,0:T(8,128)(2,1)} fusion(bf16[8,256,768]{2,1,0:T(8,128)(2,1)} %bitcast.51, s32[1024]{0:T(1024)S(1)} %pad_clamp_fusion), kind=kCustom, calls=%fused_computation | custom fusion | bytes 12582976 | tf_op jit(solution)/shard_map/gather | solution.py:45
  127.8 5.4 %broadcast.108 = f32[2,2048,768]{2,1,0:T(8,128)} broadcast(f32[]{:T(128)} %constant.102.clone.1), dimensions={} | broadcast | bytes 12582916 | tf_op jit(solution)/shard_map/broadcast.13
  133.2 5.3 %broadcast.108.clone = f32[2,2048,768]{2,1,0:T(8,128)} broadcast(f32[]{:T(128)} %constant.102.clone.1), dimensions={} | broadcast | bytes 12582916 | tf_op jit(solution)/shard_map/broadcast.13
  138.6 92.5 %while.18 = (s32[]{:T(128)}, f32[2,256,768]{2,1,0:T(8,128)S(1)}, f32[2,2048,768]{2,1,0:T(8,128)}, f32[2,2048,768]{2,1,0:T(8,128)}, bf16[2,256,768]{2,1,0:T(8,128...) while((s32[]{:T(128)}, f32[2,256,768]{2,1,0:T(8,128)S(1)}, ...), condition=%wide.region_4.5_spmd.clone, body=%wide.region_0.4_spmd.clone.sunk | while | flops 1625164800 | bytes 36614328 | solution.py:94
  138.8 2.1 fusion.73
  141.7 2.6 convolution_dynamic-update-slice_fusion.2
  144.3 2.2 fusion.74
  146.5 2.3 multiply_convert_fusion.2
  148.7 3.4 fusion.76
  152.1 1.9 fusion.75
  154.2 2.1 fusion.73
  157.0 2.6 convolution_dynamic-update-slice_fusion.2
  159.7 2.2 fusion.74
  161.8 2.3 multiply_convert_fusion.2
  164.1 3.3 fusion.76
  167.5 1.9 fusion.75
  169.5 2.1 fusion.73
  172.3 2.7 convolution_dynamic-update-slice_fusion.2
  175.0 2.2 fusion.74
  177.2 2.3 multiply_convert_fusion.2
  179.5 3.3 fusion.76
  182.8 1.9 fusion.75
  184.9 2.1 fusion.73
  187.7 2.8 convolution_dynamic-update-slice_fusion.2
  190.4 2.2 fusion.74
  192.6 2.3 multiply_convert_fusion.2
  194.9 3.4 fusion.76
  198.3 1.9 fusion.75
  200.4 2.1 fusion.73
  203.2 2.7 convolution_dynamic-update-slice_fusion.2
  205.9 2.2 fusion.74
  208.1 2.3 multiply_convert_fusion.2
  210.3 3.4 fusion.76
  213.7 1.9 fusion.75
  215.8 2.1 fusion.73
  218.6 2.6 convolution_dynamic-update-slice_fusion.2
  221.3 2.2 fusion.74
  223.4 2.3 multiply_convert_fusion.2
  225.7 3.4 fusion.76
  229.1 1.9 fusion.75
  232.2 13.2 %reshape.176 = f32[2,8,196608]{2,1,0:T(8,128)} reshape(f32[2,2048,768]{2,1,0:T(8,128)} %get-tuple-element.161) | data formatting | bytes 25165824 | tf_op jit(solution)/shard_map/reshape | solution.py:104
  245.4 7.6 %fusion.24 = bf16[8,196608]{1,0:T(8,128)(2,1)S(1)} fusion(f32[2,8,196608]{2,1,0:T(8,128)} %reshape.176, s32[2,8]{1,0:T(2,128)S(1)} %fusion.41, pred[2,8]{1,0:T(4,128)(4,1)S(1)} %iota_compare_fusion.1), kind=kOutput, calls=%fused_computation.35 | convolution fusion | flops 303563008 | bytes 15728720 | tf_op jit(solution)/shard_map/imb,imr->br/dot_general | solution.py:101
  253.0 3.2 convert_element_type.94
  256.2 13.3 %reshape.177 = f32[2,8,196608]{2,1,0:T(8,128)} reshape(f32[2,2048,768]{2,1,0:T(8,128)} %get-tuple-element.162) | data formatting | bytes 25165824 | tf_op jit(solution)/shard_map/reshape | solution.py:110
  269.6 7.6 %fusion.25 = bf16[8,196608]{1,0:T(8,128)(2,1)S(1)} fusion(f32[2,8,196608]{2,1,0:T(8,128)} %reshape.177, s32[2,8]{1,0:T(2,128)S(1)} %fusion.41, pred[2,8]{1,0:T(4,128)(4,1)S(1)} %iota_compare_fusion.1), kind=kOutput, calls=%fused_computation.36 | convolution fusion | flops 303563008 | bytes 15728720 | tf_op jit(solution)/shard_map/imb,imr->br/dot_general | solution.py:107
  277.2 3.1 convert_element_type.96
  280.3 1.4 copy-done.3
  282.8 32.6 %reduce-scatter.3.cloned.1.call-done = bf16[1,512,768]{2,1,0:T(8,128)(2,1)} async-done(((bf16[1,2048,768]{2,1,0:T(8,128)(2,1)}), bf16[1,512,768]{2,1,0:T(8,128)(2,1)}) %reduce-scatter.3.cloned.1.call-update) | async-done | bytes 786448 | tf_op jit(solution)/shard_map/reduce_scatter | solution.py:154
  315.4 1.3 multiply_reduce_fusion.1
  316.8 61.6 %reduce-scatter.5.cloned.1.call-done = bf16[1,512,768]{2,1,0:T(8,128)(2,1)} async-done(((bf16[1,2048,768]{2,1,0:T(8,128)(2,1)}), bf16[1,512,768]{2,1,0:T(8,128)(2,1)}) %reduce-scatter.5.cloned.1.call-update) | async-done | bytes 786448 | tf_op jit(solution)/shard_map/reduce_scatter | solution.py:160
  378.5 1.3 multiply_reduce_fusion
  379.9 10.4 %psum.7 = f32[6,3]{0,1:T(4,128)S(1)} all-reduce(f32[6,3]{0,1:T(4,128)S(1)} %pad_maximum_fusion), channel_id=1, replica_groups=mesh['grp'=2,'seq'=4,'head'=2,'clip'=2] {'seq'}, use_global_device_ids=true, to_apply=%region_13.14 | all-reduce | flops 18 | bytes 144 | tf_op jit(solution)/shard_map/psum | solution.py:178
  (51 shorter events, 11.4 us)
Async XLA Ops:
  7.2 25.4 %copy-start = (s32[1,8]{1,0:T(1,128)S(1)}, s32[1,8]{1,0:T(1,128)}, u32[]{:S(2)}) copy-start(s32[1,8]{1,0:T(1,128)} %param.15) | copy-start | bytes 100
  7.2 63.2 %all-gather.5.cloned.1.call-start = ((), (), s32[]{:S(2)}) async-start(), calls=%async_computation.3 | async-start | bytes 4718592 | tf_op jit(solution)/shard_map/all_gather | solution.py:136
  7.9 114.3 %all-gather.3.cloned.1.call-start = ((), (), s32[]{:S(2)}) async-start(), calls=%async_computation.2 | async-start | bytes 3932160 | tf_op jit(solution)/shard_map/all_gather | solution.py:144
  8.7 306.7 %reduce-scatter.3.cloned.1.call-start = ((), (), s32[]{:S(2)}) async-start(), calls=%async_computation.4 | async-start | bytes 3932160 | tf_op jit(solution)/shard_map/reduce_scatter | solution.py:154
  8.7 23.9 %collective-permute-start = (bf16[1,512,768]{2,1,0:T(8,128)(2,1)}, bf16[1,512,768]{2,1,0:T(8,128)(2,1)}, u32[]{:S(2)}, u32[]{:S(2)}) collective-permute-start(bf16[1,512,768]{2,1,0:T(8,128)(2,1)} %param.11), channel_id=1, source_target_pairs={{0,4},{4,8},{8,12},{12,0},{1,5},{5,9},{9,13},{13,1},{2,6},{6,10},{... | collective-permute-start | bytes 2359304 | tf_op jit(solution)/shard_map/ppermute | solution.py:23
  11.8 36.4 %collective-permute-start.1 = (bf16[1,512,768]{2,1,0:T(8,128)(2,1)}, bf16[1,512,768]{2,1,0:T(8,128)(2,1)}, u32[]{:S(2)}, u32[]{:S(2)}) collective-permute-start(bf16[1,512,768]{2,1,0:T(8,128)(2,1)} %param.11), channel_id=1, source_target_pairs={{0,12},{4,0},{8,4},{12,8},{1,13},{5,1},{9,5},{13,9},{2,14},{6,2},{... | collective-permute-start | bytes 2359304 | tf_op jit(solution)/shard_map/ppermute | solution.py:28
  32.6 32.9 %collective-permute-start.2 = (bf16[1,512,768]{2,1,0:T(8,128)(2,1)}, bf16[1,512,768]{2,1,0:T(8,128)(2,1)}, u32[]{:S(2)}, u32[]{:S(2)}) collective-permute-start(bf16[1,512,768]{2,1,0:T(8,128)(2,1)} %collective-permute-done), channel_id=1, source_target_pairs={{0,4},{4,8},{8,12},{12,0},{1,5},{5,9},{9,13},{13,1},{2,6},{6,10},{... | collective-permute-start | bytes 2359304 | tf_op jit(solution)/shard_map/ppermute | solution.py:23
  231.0 1.1 copy-start.2
  256.2 122.3 %reduce-scatter.5.cloned.1.call-start = ((), (), s32[]{:S(2)}) async-start(), calls=%async_computation.5 | async-start | bytes 3932160 | tf_op jit(solution)/shard_map/reduce_scatter | solution.py:160
  277.2 113.7 %copy-start.1 = (s32[1,8]{1,0:T(1,128)S(1)}, s32[1,8]{1,0:T(1,128)}, u32[]{:S(2)}) copy-start(s32[1,8]{1,0:T(1,128)} %param.15) | copy-start | bytes 100
  280.3 1.4 copy-start.3
Sparse Core Ops, SparseCore 0:
  9.5 47.6 all-gather.4
  58.8 63.4 all-gather.2
  256.3 59.0 reduce-scatter.2
  318.1 60.2 reduce-scatter.4
